TPU v7x, 32 devices: a whole 2x2x4 slice. The times are simulated.
32 devices in a mesh: dp: 4 (over y, core), mp: 8 (over z, x).
Axes of the slice: x: 2, y: 2, z: 4, core: 2. Of those that a mesh axis runs over, the one named last changes fastest.
Arguments:
- pair_tokens: bfloat16 [64, 48, 8192], P('dp', None, 'mp'), may hold values from -6 to 6
- norm_gain: float32 [8192], replicated, may hold values from 0.1 to 1.9
- q_weight: bfloat16 [8192, 4096], P('dp', 'mp'), may hold values from -1.5 to 1.5
- k_weight: bfloat16 [8192, 1024], P('dp', 'mp'), may hold values from -1.5 to 1.5
- value_weight: bfloat16 [8192, 1024], P('dp', 'mp'), may hold values from -0.0625 to 0.0625
- o_weight: bfloat16 [4096, 8192], P('mp', 'dp'), may hold values from -0.375 to 0.375
- pair_row: int32 [64], replicated, may hold values from 0 to 15, as said below
- pair_span: int32 [64, 2], replicated, may hold values from 0 to 128, as said below
- block_ids: int32 [2048], P('dp'), may hold values from 0 to 11, as said below
Outputs:
- attn_out: bfloat16 [2048, 8192], P('dp', 'mp')
Inputs may be any that keep to these rules, and one draw needn't show every extreme that they name: `pair_row`: every packed row is tiled exactly by the spans of the pairs that name it; the pairs listed on one index of dp that name rows of one index of dp number at most 4, and 4 is reached. `pair_span`: each span holds one pair, start before end; end - start is at least 3 and at most 48; 48 is reached in every row, and the last pair of every row ends at 128. `block_ids`: the pair's place counts the pairs of its row in order of position; roles are 0 prompt, 1 chosen, 2 rejected, in that order within each pair, each present; consistent with pair_row and pair_span.
All inputs are finite; a program needn't handle non-finite values.
Results may differ from a plain program's by a relative error of at most 0.013.
Values may be sent and summed in bfloat16 or wider, within the bound.
A program may use at most 128 MiB of HBM per device.

v0:
```python
import jax
import jax.numpy as jnp
from jax import lax
from jax.sharding import PartitionSpec as P

HEAD_SIZE = 128
ROW_TOKENS = 128
QUERY_PER_KV = 4


def apply_rotary(values, token_position, heads):
    half = HEAD_SIZE // 2
    freq = 500000.0 ** (-(jnp.arange(half, dtype=jnp.float32) * 2.0 / HEAD_SIZE))
    angle = token_position.astype(jnp.float32)[:, None] * freq[None, :]
    cosine = jnp.cos(angle)[:, None, :]
    sine = jnp.sin(angle)[:, None, :]
    shaped = values.reshape(values.shape[0], heads, HEAD_SIZE)
    first = shaped[..., :half]
    second = shaped[..., half:]
    turned = jnp.concatenate(
        [first * cosine - second * sine, second * cosine + first * sine], axis=-1
    )
    return turned.reshape(values.shape[0], heads * HEAD_SIZE).astype(jnp.bfloat16)


def row_mask(ids):
    pair_of = ids // 3
    role_of = ids % 3
    steps_a = jnp.arange(ids.shape[0])
    causal = steps_a[None, :] <= steps_a[:, None]
    same = pair_of[:, None] == pair_of[None, :]
    hidden_pair = (role_of[:, None] == 2) & (role_of[None, :] == 1)
    return causal & same & jnp.logical_not(hidden_pair)


def local(
    pair_tokens,
    norm_gain,
    q_weight,
    k_weight,
    value_weight,
    o_weight,
    pair_row,
    pair_span,
    block_ids,
):
    dp_count = lax.axis_size("dp")
    own_index = lax.axis_index("dp")
    pairs_dev = pair_tokens.shape[0]
    pair_cap = pair_tokens.shape[1]
    width_local = pair_tokens.shape[2]
    all_pairs = pair_row.shape[0]
    most_sent = -(-pairs_dev // dp_count)
    tok_dev = block_ids.shape[0]
    rows_dev = tok_dev // ROW_TOKENS
    owners_all = (pair_row // rows_dev).reshape(dp_count, pairs_dev)
    same_owner = owners_all[:, :, None] == owners_all[:, None, :]
    listed = jnp.arange(pairs_dev)
    before = listed[None, :] < listed[:, None]
    rank_all = jnp.sum((same_owner & before[None]).astype(jnp.int32), axis=2)
    own_owner = lax.dynamic_index_in_dim(owners_all, own_index, 0, keepdims=False)
    own_rank = lax.dynamic_index_in_dim(rank_all, own_index, 0, keepdims=False)
    outgoing = jnp.zeros((dp_count * most_sent, pair_cap, width_local), jnp.bfloat16)
    outgoing = outgoing.at[own_owner * most_sent + own_rank].set(pair_tokens)
    incoming = lax.all_to_all(
        outgoing.reshape(dp_count, most_sent * pair_cap, width_local),
        "dp",
        split_axis=0,
        concat_axis=0,
        tiled=True,
    )
    slots = jnp.arange(pair_cap, dtype=jnp.int32)
    length = pair_span[:, 1] - pair_span[:, 0]
    source = jnp.arange(all_pairs, dtype=jnp.int32) // pairs_dev
    target = (pair_row % rows_dev)[:, None] * ROW_TOKENS + pair_span[:, 0][:, None] + slots[None, :]
    usable = (owners_all.reshape(-1) == own_index)[:, None] & (slots[None, :] < length[:, None])
    slot_index = (source * most_sent + rank_all.reshape(-1))[:, None] * pair_cap + slots[None, :]
    buffer_size = dp_count * most_sent * pair_cap
    slot_index = jnp.where(usable, slot_index, buffer_size)
    placement_map = jnp.full((buffer_size,), tok_dev, jnp.int32)
    placement_map = placement_map.at[slot_index.reshape(-1)].set(target.reshape(-1), mode="drop")
    packed_local = jnp.zeros((tok_dev, width_local), jnp.bfloat16)
    packed_local = packed_local.at[placement_map].set(
        incoming.reshape(buffer_size, width_local), mode="drop"
    )
    packed = lax.all_gather(packed_local, "mp", axis=1, tiled=True)
    wide = packed.astype(jnp.float32)
    scale = lax.rsqrt(jnp.mean(wide * wide, axis=-1, keepdims=True) + 1e-05)
    normed = (wide * scale * norm_gain[None, :]).astype(jnp.bfloat16)

    def add_rows(piece):
        return jnp.dot(normed, piece, preferred_element_type=jnp.float32)

    query_heads = add_rows(lax.all_gather(q_weight, "dp", axis=0, tiled=True))
    key_rows = add_rows(lax.all_gather(k_weight, "dp", axis=0, tiled=True))
    value_sum = add_rows(lax.all_gather(value_weight, "dp", axis=0, tiled=True))
    value_heads = value_sum.astype(jnp.bfloat16)
    ids_rows = block_ids.reshape(rows_dev, ROW_TOKENS)
    visible = jax.vmap(row_mask)(ids_rows)
    token_position = (jnp.sum(visible.astype(jnp.int32), axis=2) - 1).reshape(tok_dev)
    kv_local = k_weight.shape[1] // HEAD_SIZE
    q_local = q_weight.shape[1] // HEAD_SIZE
    rotated_query = apply_rotary(query_heads, token_position, q_local).reshape(
        rows_dev, ROW_TOKENS, kv_local, QUERY_PER_KV, HEAD_SIZE
    )
    rotated_key = apply_rotary(key_rows, token_position, kv_local).reshape(
        rows_dev, ROW_TOKENS, kv_local, HEAD_SIZE
    )
    v_rows = value_heads.reshape(rows_dev, ROW_TOKENS, kv_local, HEAD_SIZE)
    scores = jnp.einsum(
        "rihgd,rjhd->rhgij", rotated_query, rotated_key, preferred_element_type=jnp.float32
    ) * HEAD_SIZE ** (-0.5)
    scores = jnp.where(visible[:, None, None], scores, -1e30)
    top = jnp.max(scores, axis=-1, keepdims=True)
    expo = jnp.exp(scores - top)
    probs = (expo / jnp.sum(expo, axis=-1, keepdims=True)).astype(jnp.bfloat16)
    attn = jnp.einsum(
        "rhgij,rjhd->rihgd", probs, v_rows, preferred_element_type=jnp.float32
    ).astype(jnp.bfloat16)
    attn = attn.reshape(tok_dev, q_local * HEAD_SIZE)
    terms = jnp.dot(
        attn, lax.all_gather(o_weight, "dp", axis=1, tiled=True), preferred_element_type=jnp.float32
    )
    return lax.psum_scatter(terms.astype(jnp.bfloat16), "mp", scatter_dimension=1, tiled=True)


def solution(mesh):
    placed = (
        P("dp", None, "mp"),
        P(),
        P("dp", "mp"),
        P("dp", "mp"),
        P("dp", "mp"),
        P("mp", "dp"),
        P(),
        P(),
        P("dp"),
    )
    return jax.shard_map(
        local, mesh=mesh, in_specs=placed, out_specs=P("dp", "mp"), check_vma=False
    )
```

profile of v0, /device:TPU:0, one launch (start us, length us, event | category | flops | bytes accessed | tf_op | source)
XLA Modules:
  0.0 501.9 jit_solution(16550077983021786801)
XLA Ops:
  6.6 0.7 broadcast_compare_fusion.2
  7.6 1.3 broadcast_in_dim.24
  8.9 5.4 %scatter_fusion = bf16[16,48,1024]{2,1,0:T(8,128)(2,1)} fusion(bf16[16,48,1024]{2,1,0:T(8,128)(2,1)} %broadcast_in_dim.24, s32[16]{0:T(128)S(1)} %fusion.33, bf16[16,48,1024]{2,1,0:T(8,128)(2,1)} %param.9), kind=kCustom, calls=%fused_computation.1 | custom fusion | bytes 4718656 | tf_op jit(solution)/shard_map/scatter | solution.py:64
  14.4 4.3 all-to-all-start
  19.1 11.8 %scatter_custom_fusion = s32[768]{0:T(1024)S(1)} fusion(s32[3072]{0:T(1024)S(1)} %bitcast.87, s32[3072]{0:T(1024)S(1)} %reshape.406, s32[]{:T(128)} %constant.90.clone.1), kind=kCustom, calls=%fused_computation.60 | custom fusion | bytes 3076 | tf_op jit(solution)/shard_map/scatter | solution.py:81
  30.9 7.8 %all-to-all-done = bf16[4,192,1024]{2,1,0:T(8,128)(2,1)S(1)} async-done(((bf16[4,192,1024]{2,1,0:T(8,128)(2,1)}), bf16[4,192,1024]{2,1,0:T(8,128)(2,1)S(1)}, u32[]{:S(2)}, u32[]{:S(2)}) %all-to-all-start) | async-done | bytes 1572896 | tf_op jit(solution)/shard_map/all_to_all | solution.py:65
  38.7 6.7 %scatter_custom_fusion.2 = bf16[512,1024]{1,0:T(8,128)(2,1)} fusion(s32[768]{0:T(1024)S(1)} %compare_select_fusion.1, bf16[768,1024]{1,0:T(8,128)(2,1)S(1)} %bitcast.83, bf16[]{:T(256)} %constant.89.clone.1), kind=kCustom, calls=%fused_computation.26 | custom fusion | bytes 1048578 | tf_op jit(solution)/shard_map/scatter | solution.py:83
  45.4 0.7 all-gather.12.cloned.1.call-update
  46.1 0.7 all-gather.10.cloned.1.call-update
  46.9 0.5 all-gather.8.cloned.1.call-update
  47.5 0.5 all-gather.14.cloned.1.call-update
  48.4 1.0 multiply_cosine_fusion
  49.4 121.7 %all-gather.6.cloned.1.call-done = bf16[512,8192]{1,0:T(8,128)(2,1)} async-done(((bf16[512,1024]{1,0:T(8,128)(2,1)}), bf16[512,8192]{1,0:T(8,128)(2,1)}) %all-gather.6.cloned.1.call-update) | async-done | bytes 8388624 | tf_op jit(solution)/shard_map/all_gather | solution.py:86
  171.0 5.1 %fusion = f32[512]{0:T(512)S(1)} fusion(bf16[512,8192]{1,0:T(8,128)(2,1)} %all-gather.6.cloned.1.call-done), kind=kLoop, calls=%fused_computation.5 | loop fusion | flops 12582400 | bytes 8390656 | tf_op jit(solution)/shard_map/reduce_sum | solution.py:88
  176.1 52.9 %all-gather.12.cloned.1.call-done = bf16[8192,512]{1,0:T(8,128)(2,1)} async-done(((bf16[2048,512]{1,0:T(8,128)(2,1)}), bf16[8192,512]{1,0:T(8,128)(2,1)}) %all-gather.12.cloned.1.call-update) | async-done | bytes 8388624 | tf_op jit(solution)/shard_map/all_gather | solution.py:94
  229.0 11.4 %fusion.35 = f32[512,512]{0,1:T(8,128)S(1)} fusion(bf16[8192,512]{1,0:T(8,128)(2,1)} %all-gather.12.cloned.1.call-done, bf16[512,8192]{1,0:T(8,128)(2,1)} %all-gather.6.cloned.1.call-done, f32[8192]{0:T(1024)S(1)} %copy-done.3, f32[512]{0:T(512)S(1)} %add_rsqrt_fusion), kind=kOutput, calls=%fused_computation.87 | convolution fusion | flops 4311744512 | bytes 17860608 | tf_op jit(solution)/shard_map/dot_general | solution.py:92
  241.2 12.1 %all-gather.10.cloned.1.call-done = bf16[8192,128]{1,0:T(8,128)(2,1)} async-done(((bf16[2048,128]{1,0:T(8,128)(2,1)}), bf16[8192,128]{1,0:T(8,128)(2,1)}) %all-gather.10.cloned.1.call-update) | async-done | bytes 2097168 | tf_op jit(solution)/shard_map/all_gather | solution.py:95
  253.2 6.5 %convolution_bitcast_fusion = f32[512,1,128]{0,2,1:T(8,128)S(1)} fusion(bf16[8192,128]{1,0:T(8,128)(2,1)} %all-gather.10.cloned.1.call-done, bf16[512,8192]{1,0:T(8,128)(2,1)} %all-gather.6.cloned.1.call-done, f32[8192]{0:T(1024)S(1)} %copy-done.3, f32[512]{0:T(512)S(1)} %add_rsqrt_fusion), kind=kOutput, calls=%fused_computation.14 | convolution fusion | flops 1090519040 | bytes 10782720 | tf_op jit(solution)/shard_map/dot_general | solution.py:92
  259.7 0.6 fusion.18
  261.5 15.7 %all-gather.8.cloned.1.call-done = bf16[8192,128]{1,0:T(8,128)(2,1)} async-done(((bf16[2048,128]{1,0:T(8,128)(2,1)}), bf16[8192,128]{1,0:T(8,128)(2,1)}) %all-gather.8.cloned.1.call-update) | async-done | bytes 2097168 | tf_op jit(solution)/shard_map/all_gather | solution.py:96
  277.2 6.4 %convolution_convert_fusion.2 = bf16[512,128]{1,0:T(8,128)(2,1)S(1)} fusion(bf16[8192,128]{1,0:T(8,128)(2,1)} %all-gather.8.cloned.1.call-done, bf16[512,8192]{1,0:T(8,128)(2,1)} %all-gather.6.cloned.1.call-done, f32[8192]{0:T(1024)S(1)} %copy-done.3, f32[512]{0:T(512)S(1)} %add_rsqrt_fusion), kind=kOutput, calls=%fused_computation.15 | convolution fusion | flops 1090584576 | bytes 10651648 | tf_op jit(solution)/shard_map/dot_general | solution.py:92
  284.3 52.7 %all-gather.14.cloned.1.call-done = bf16[512,8192]{1,0:T(8,128)(2,1)} async-done(((bf16[512,2048]{1,0:T(8,128)(2,1)}), bf16[512,8192]{1,0:T(8,128)(2,1)}) %all-gather.14.cloned.1.call-update) | async-done | bytes 8388624 | tf_op jit(solution)/shard_map/all_gather | solution.py:122
  336.9 10.1 %convolution_convert_fusion = bf16[512,8192]{1,0:T(8,128)(2,1)} fusion(bf16[512,8192]{1,0:T(8,128)(2,1)} %all-gather.14.cloned.1.call-done, bf16[64,8,4,128]{3,2,1,0:T(4,128)(2,1)S(1)} %bitcast.86), kind=kOutput, calls=%fused_computation.8 | convolution fusion | flops 4299161600 | bytes 17301504 | tf_op jit(solution)/shard_map/dot_general | solution.py:121
  347.0 148.0 %reduce-scatter.2.cloned.1.call-done = bf16[512,1024]{1,0:T(8,128)(2,1)} async-done(((bf16[512,8192]{1,0:T(8,128)(2,1)}), bf16[512,1024]{1,0:T(8,128)(2,1)}) %reduce-scatter.2.cloned.1.call-update) | async-done | bytes 1048592 | tf_op jit(solution)/shard_map/reduce_scatter | solution.py:124
  (47 shorter events, 3.9 us)
Async XLA Ops:
  6.5 12.2 %copy-start.1 = (s32[64]{0:T(128)S(1)}, s32[64]{0:T(128)}, u32[]{:S(2)}) copy-start(s32[64]{0:T(128)} %param.15) | copy-start | bytes 772
  6.5 12.2 %copy-start.2 = (s32[64,2]{0,1:T(2,128)S(1)}, s32[64,2]{0,1:T(2,128)}, u32[]{:S(2)}) copy-start(s32[64,2]{0,1:T(2,128)} %param.16) | copy-start | bytes 1540
  7.6 40.5 %copy-start = (s32[512]{0:T(512)S(1)}, s32[512]{0:T(512)}, u32[]{:S(2)}) copy-start(s32[512]{0:T(512)} %param.17) | copy-start | bytes 6148
  14.4 24.3 %all-to-all-start = ((bf16[4,192,1024]{2,1,0:T(8,128)(2,1)}), bf16[4,192,1024]{2,1,0:T(8,128)(2,1)S(1)}, u32[]{:S(2)}, u32[]{:S(2)}) async-start(bf16[4,192,1024]{2,1,0:T(8,128)(2,1)} %bitcast.6), calls=%async_computation | async-start | bytes 3145728 | tf_op jit(solution)/shard_map/all_to_all | solution.py:65
  18.6 210.4 %copy-start.3 = (f32[8192]{0:T(1024)S(1)}, f32[8192]{0:T(1024)}, u32[]{:S(2)}) copy-start(f32[8192]{0:T(1024)} %param.10) | copy-start | bytes 98308
  18.6 152.4 %all-gather.6.cloned.1.call-start = ((), (), s32[]{:S(2)}) async-start(), calls=%async_computation.2 | async-start | bytes 9437184 | tf_op jit(solution)/shard_map/all_gather | solution.py:86
  45.3 183.7 %all-gather.12.cloned.1.call-start = ((), (), s32[]{:S(2)}) async-start(), calls=%async_computation.5 | async-start | bytes 10485760 | tf_op jit(solution)/shard_map/all_gather | solution.py:94
  46.1 207.1 %all-gather.10.cloned.1.call-start = ((), (), s32[]{:S(2)}) async-start(), calls=%async_computation.4 | async-start | bytes 2621440 | tf_op jit(solution)/shard_map/all_gather | solution.py:95
  46.8 230.4 %all-gather.8.cloned.1.call-start = ((), (), s32[]{:S(2)}) async-start(), calls=%async_computation.3 | async-start | bytes 2621440 | tf_op jit(solution)/shard_map/all_gather | solution.py:96
  47.4 289.5 %all-gather.14.cloned.1.call-start = ((), (), s32[]{:S(2)}) async-start(), calls=%async_computation.6 | async-start | bytes 10485760 | tf_op jit(solution)/shard_map/all_gather | solution.py:122
  48.0 447.0 %reduce-scatter.2.cloned.1.call-start = ((), (), s32[]{:S(2)}) async-start(), calls=%async_computation.7 | async-start | bytes 9437184 | tf_op jit(solution)/shard_map/reduce_scatter | solution.py:124
Sparse Core Ops, SparseCore 0:
  45.5 125.4 all-gather.5
  172.6 56.4 all-gather.11
  230.6 22.5 all-gather.9
  254.7 22.5 all-gather.7
  278.6 58.2 all-gather.13
  347.2 147.8 reduce-scatter.1
where the time goes:
time: 502 us
  waiting for transfers between devices  413 us (82%)
  matrix products  35 us (7%)
  local copies, waits for them, and re-layouts  26.7 us (5%)
  between operations  13.7 us (3%)
  other arithmetic  8.88 us (2%)
    reduce_scatter x1, waiting for transfers between devices, local(): lax.psum_scatter(terms.astype(jnp.bfloat16), 'mp', scatter_dimension=1, t...  148 us
    all_gather x1, waiting for transfers between devices, local(): packed = lax.all_gather(packed_local, 'mp', axis=1, tiled=True)  122 us
    all_gather x1, waiting for transfers between devices, local(): query_heads = add_rows(lax.all_gather(q_weight, 'dp', axis=0, tiled=True))  52.9 us
    all_gather x1, waiting for transfers between devices, local(): lax.all_gather(o_weight, 'dp', axis=1, tiled=True)  52.7 us
    dot_general x3, matrix products, add_rows(): return jnp.dot(normed, piece, preferred_element_type=jnp.float32)  24.2 us
    all_gather x1, waiting for transfers between devices, local(): value_sum = add_rows(lax.all_gather(value_weight, 'dp', axis=0, tiled=True))  15.7 us
    all_gather x1, waiting for transfers between devices, local(): key_rows = add_rows(lax.all_gather(k_weight, 'dp', axis=0, tiled=True))  12.1 us
    scatter x1, local copies, waits for them, and re-layouts, local(): placement_map.at[slot_index.reshape(-1)]  11.8 us
  transfers between devices with their start and end apart: 7, of which 7 were waited for; matrix products, arithmetic and copies ran while one was open for 9% of the time, Pallas kernels for 0%

commit v1 on v0

--- a/solution.py
+++ b/solution.py
@@ -6,6 +6,28 @@
 HEAD_SIZE = 128
 ROW_TOKENS = 128
 QUERY_PER_KV = 4
+
+
+def laid_out(blocks, dim):
+    blocks = jnp.moveaxis(blocks, 0, dim)
+    shape = blocks.shape
+    return blocks.reshape(*shape[:dim], shape[dim] * shape[dim + 1], *shape[dim + 2 :])
+
+
+def doubled(x, axis):
+    devices = lax.axis_size(axis)
+    tiles = x[None]
+    for level in range(devices.bit_length() - 1):
+        bit = 1 << level
+        other = lax.ppermute(tiles, axis, [(i, i ^ bit) for i in range(devices)])
+        both = jnp.stack([tiles, other])
+        upper = lax.axis_index(axis) >> level & 1
+        tiles = jnp.where(upper == 0, both, both[::-1]).reshape(-1, *x.shape)
+    return tiles
+
+
+def doubled_up(shard, axis, dim):
+    return laid_out(doubled(shard, axis), dim)
 
 
 def apply_rotary(values, token_position, heads):
@@ -91,7 +113,7 @@
     def add_rows(piece):
         return jnp.dot(normed, piece, preferred_element_type=jnp.float32)
 
-    query_heads = add_rows(lax.all_gather(q_weight, "dp", axis=0, tiled=True))
+    query_heads = add_rows(doubled_up(q_weight, "dp", 0))
     key_rows = add_rows(lax.all_gather(k_weight, "dp", axis=0, tiled=True))
     value_sum = add_rows(lax.all_gather(value_weight, "dp", axis=0, tiled=True))
     value_heads = value_sum.astype(jnp.bfloat16)

time: 502 us -> 444 us (0.88)
  waiting for transfers between devices: 413 us -> 320 us
  other arithmetic: 8.88 us -> 33.5 us
  local copies, waits for them, and re-layouts: 26.7 us -> 38.7 us
    all_gather x1, waiting for transfers between devices: 122 us -> 0.01 us  [local(): packed = lax.all_gather(packed_local, 'mp', axis=1, tiled=True)]
    ppermute x0 -> x2, waiting for transfers between devices: none -> 95.9 us  [doubled(): other = lax.ppermute(tiles, axis, [(i, i ^ bit) for i in range(devices)])]
    all_gather x1 -> x0, waiting for transfers between devices: 52.9 us -> none  [local(): query_heads = add_rows(lax.all_gather(q_weight, 'dp', axis=0, tiled=True))]
    another operation x2 -> x5, other arithmetic: 0.87 us -> 14.6 us  [the longest x3 13.8 us: doubled(): both = jnp.stack([tiles, other])]
    dot_general x0 -> x1, local copies, waits for them, and re-layouts: none -> 12 us  [add_rows(): return jnp.dot(normed, piece, preferred_element_type=jnp.float32)]
    select_n x0 -> x1, other arithmetic: none -> 11.6 us  [doubled(): tiles = jnp.where(upper == 0, both, both[::-1]).reshape(-1, *x.shape)]
    all_gather x1, waiting for transfers between devices: 15.7 us -> 6.11 us  [local(): value_sum = add_rows(lax.all_gather(value_weight, 'dp', axis=0, tiled=True))]
    all_gather x1, waiting for transfers between devices: 12.1 us -> 6.56 us  [local(): key_rows = add_rows(lax.all_gather(k_weight, 'dp', axis=0, tiled=True))]
  transfers between devices with their start and end apart: 7 -> 8, of which waited for: 7 -> 7; matrix products, arithmetic and copies ran while one was open for 9% -> 18% of each run, Pallas kernels for 0% -> 0%
where the time goes in v1:
time: 444 us
  waiting for transfers between devices  320 us (72%)
  local copies, waits for them, and re-layouts  38.7 us (9%)
  matrix products  33.8 us (8%)
  other arithmetic  33.5 us (8%)
  between operations  13.4 us (3%)
  starting transfers between devices  4.6 us (1%)
    reduce_scatter x1, waiting for transfers between devices, local(): lax.psum_scatter(terms.astype(jnp.bfloat16), 'mp', scatter_dimension=1, t...  148 us
    ppermute x2, waiting for transfers between devices, doubled(): other = lax.ppermute(tiles, axis, [(i, i ^ bit) for i in range(devices)])  95.9 us
    all_gather x1, waiting for transfers between devices, local(): lax.all_gather(o_weight, 'dp', axis=1, tiled=True)  52.7 us
    dot_general x3, matrix products, add_rows(): return jnp.dot(normed, piece, preferred_element_type=jnp.float32)  23 us
    another operation x3, other arithmetic, doubled(): both = jnp.stack([tiles, other])  13.8 us
    dot_general x1, local copies, waits for them, and re-layouts, add_rows(): return jnp.dot(normed, piece, preferred_element_type=jnp.float32)  12 us
    scatter x1, local copies, waits for them, and re-layouts, local(): placement_map.at[slot_index.reshape(-1)]  11.8 us
    select_n x1, other arithmetic, doubled(): tiles = jnp.where(upper == 0, both, both[::-1]).reshape(-1, *x.shape)  11.6 us
  transfers between devices with their start and end apart: 8, of which 7 were waited for; matrix products, arithmetic and copies ran while one was open for 18% of the time, Pallas kernels for 0%

profile of v1, /device:TPU:0, one launch (start us, length us, event | category | flops | bytes accessed | tf_op | source)
XLA Modules:
  0.0 443.6 jit_solution(13951629586997957536)
XLA Ops:
  6.6 0.8 broadcast_compare_fusion.2
  7.7 1.3 broadcast_in_dim.26
  9.0 5.5 %scatter_fusion = bf16[16,48,1024]{2,1,0:T(8,128)(2,1)} fusion(bf16[16,48,1024]{2,1,0:T(8,128)(2,1)} %broadcast_in_dim.26, s32[16]{0:T(128)S(1)} %fusion.38, bf16[16,48,1024]{2,1,0:T(8,128)(2,1)} %param.9), kind=kCustom, calls=%fused_computation.1 | custom fusion | bytes 4718656 | tf_op jit(solution)/shard_map/scatter | solution.py:86
  14.5 4.3 all-to-all-start
  19.4 11.8 %scatter_custom_fusion = s32[768]{0:T(1024)S(1)} fusion(s32[3072]{0:T(1024)S(1)} %bitcast.110, s32[3072]{0:T(1024)S(1)} %reshape.408, s32[]{:T(128)} %constant.91.clone.1), kind=kCustom, calls=%fused_computation.69 | custom fusion | bytes 3076 | tf_op jit(solution)/shard_map/scatter | solution.py:103
  31.2 8.5 %all-to-all-done = bf16[4,192,1024]{2,1,0:T(8,128)(2,1)} async-done(((bf16[4,192,1024]{2,1,0:T(8,128)(2,1)}), bf16[4,192,1024]{2,1,0:T(8,128)(2,1)}, u32[]{:S(2)}, u32[]{:S(2)}) %all-to-all-start) | async-done | bytes 1572896 | tf_op jit(solution)/shard_map/all_to_all | solution.py:87
  39.7 7.3 %scatter_custom_fusion.2 = bf16[512,1024]{1,0:T(8,128)(2,1)} fusion(s32[768]{0:T(1024)S(1)} %compare_select_fusion.1, bf16[768,1024]{1,0:T(8,128)(2,1)} %bitcast.7, bf16[]{:T(256)} %constant.90.clone.1), kind=kCustom, calls=%fused_computation.35 | custom fusion | bytes 1049088 | tf_op jit(solution)/shard_map/scatter | solution.py:105
  47.1 0.7 all-gather.9.cloned.1.call-update
  49.2 3.8 collective-permute-done
  52.9 2.0 pad_maximum_fusion.1
  54.9 4.4 fusion.6
  60.2 92.1 %collective-permute-done.1 = bf16[2,2048,512]{2,1,0:T(8,128)(2,1)} collective-permute-done((bf16[2,2048,512]{2,1,0:T(8,128)(2,1)}, bf16[2,2048,512]{2,1,0:T(8,128)(2,1)}, u32[]{:S(2)}, u32[]{:S(2)}) %collective-permute-start.1) | collective-permute-done | bytes 4194336 | tf_op jit(solution)/shard_map/ppermute | solution.py:22
  152.3 7.5 %pad_maximum_fusion = bf16[2,2,2048,512]{3,2,1,0:T(8,128)(2,1)} fusion(bf16[1,2,2048,512]{3,2,1,0:T(8,128)(2,1)} %bitcast.24, bf16[1,2,2048,512]{3,2,1,0:T(8,128)(2,1)} %get-tuple-element.9), kind=kLoop, calls=%fused_computation.10 | loop fusion | flops 4194304 | bytes 16777216 | tf_op jit(solution)/shard_map/stack | solution.py:23
  159.7 11.6 %reverse_select_fusion = bf16[2,2,2048,512]{3,2,1,0:T(8,128)(2,1)} fusion(bf16[2,2,2048,512]{3,2,1,0:T(8,128)(2,1)} %pad_maximum_fusion, pred[]{:T(512)S(6)} %eq.80), kind=kLoop, calls=%fused_computation.8 | loop fusion | flops 4194304 | bytes 16777216 | tf_op jit(solution)/shard_map/jit(_where)/select_n | solution.py:25
  171.3 12.0 %copy.21 = bf16[512,8192]{1,0:T(8,128)(2,1)} copy(bf16[512,8192]{0,1:T(8,128)(2,1)} %bitcast.104) | data formatting | bytes 16777216 | tf_op jit(solution)/shard_map/dot_general | solution.py:114
  183.3 5.1 %fusion = f32[512]{0:T(512)S(1)} fusion(bf16[512,8192]{1,0:T(8,128)(2,1)} %all-gather.5.cloned.1.call-done), kind=kLoop, calls=%fused_computation.5 | loop fusion | flops 12582400 | bytes 8390656 | tf_op jit(solution)/shard_map/reduce_sum | solution.py:110
  188.5 6.6 %all-gather.9.cloned.1.call-done = bf16[8192,128]{1,0:T(8,128)(2,1)} async-done(((bf16[2048,128]{1,0:T(8,128)(2,1)}), bf16[8192,128]{1,0:T(8,128)(2,1)}) %all-gather.9.cloned.1.call-update) | async-done | bytes 2097168 | tf_op jit(solution)/shard_map/all_gather | solution.py:117
  195.0 6.5 %convolution_bitcast_fusion = f32[512,1,128]{0,2,1:T(8,128)S(1)} fusion(bf16[8192,128]{1,0:T(8,128)(2,1)} %all-gather.9.cloned.1.call-done, bf16[512,8192]{1,0:T(8,128)(2,1)} %all-gather.5.cloned.1.call-done, f32[8192]{0:T(1024)S(1)} %copy-done.4, f32[512]{0:T(512)S(1)} %add_rsqrt_fusion), kind=kOutput, calls=%fused_computation.22 | convolution fusion | flops 1090519040 | bytes 10782720 | tf_op jit(solution)/shard_map/dot_general | solution.py:114
  202.2 10.2 %fusion.3 = f32[512,4,128]{0,2,1:T(8,128)S(1)} fusion(bf16[4,128,8192]{2,1,0:T(8,128)(2,1)} %bitcast.105, bf16[512,8192]{1,0:T(8,128)(2,1)} %all-gather.5.cloned.1.call-done, f32[8192]{0:T(1024)S(1)} %copy-done.4, f32[512]{0:T(512)S(1)} %add_rsqrt_fusion), kind=kOutput, calls=%fused_computation.11 | convolution fusion | flops 4311744512 | bytes 17860608 | tf_op jit(solution)/shard_map/dot_general | solution.py:114
  213.1 6.1 %all-gather.7.cloned.1.call-done = bf16[8192,128]{1,0:T(8,128)(2,1)} async-done(((bf16[2048,128]{1,0:T(8,128)(2,1)}), bf16[8192,128]{1,0:T(8,128)(2,1)}) %all-gather.7.cloned.1.call-update) | async-done | bytes 2097168 | tf_op jit(solution)/shard_map/all_gather | solution.py:118
  219.2 6.4 %convolution_convert_fusion.2 = bf16[512,128]{1,0:T(8,128)(2,1)S(1)} fusion(bf16[8192,128]{1,0:T(8,128)(2,1)} %all-gather.7.cloned.1.call-done, bf16[512,8192]{1,0:T(8,128)(2,1)} %all-gather.5.cloned.1.call-done, f32[8192]{0:T(1024)S(1)} %copy-done.4, f32[512]{0:T(512)S(1)} %add_rsqrt_fusion), kind=kOutput, calls=%fused_computation.23 | convolution fusion | flops 1090584576 | bytes 10651648 | tf_op jit(solution)/shard_map/dot_general | solution.py:114
  226.2 52.7 %all-gather.11.cloned.1.call-done = bf16[512,8192]{1,0:T(8,128)(2,1)} async-done(((bf16[512,2048]{1,0:T(8,128)(2,1)}), bf16[512,8192]{1,0:T(8,128)(2,1)}) %all-gather.11.cloned.1.call-update) | async-done | bytes 8388624 | tf_op jit(solution)/shard_map/all_gather | solution.py:144
  278.9 10.1 %convolution_convert_fusion = bf16[512,8192]{1,0:T(8,128)(2,1)} fusion(bf16[512,8192]{1,0:T(8,128)(2,1)} %all-gather.11.cloned.1.call-done, bf16[64,8,4,128]{3,2,1,0:T(4,128)(2,1)S(1)} %bitcast.108), kind=kOutput, calls=%fused_computation.9 | convolution fusion | flops 4299161600 | bytes 17301504 | tf_op jit(solution)/shard_map/dot_general | solution.py:143
  289.1 148.0 %reduce-scatter.2.cloned.1.call-done = bf16[512,1024]{1,0:T(8,128)(2,1)} async-done(((bf16[512,8192]{1,0:T(8,128)(2,1)}), bf16[512,1024]{1,0:T(8,128)(2,1)}) %reduce-scatter.2.cloned.1.call-update) | async-done | bytes 1048592 | tf_op jit(solution)/shard_map/reduce_scatter | solution.py:146
  (51 shorter events, 5.0 us)
Async XLA Ops:
  6.5 12.4 %copy-start.2 = (s32[64]{0:T(128)S(1)}, s32[64]{0:T(128)}, u32[]{:S(2)}) copy-start(s32[64]{0:T(128)} %param.15) | copy-start | bytes 772
  6.5 12.4 %copy-start.3 = (s32[64,2]{0,1:T(2,128)S(1)}, s32[64,2]{0,1:T(2,128)}, u32[]{:S(2)}) copy-start(s32[64,2]{0,1:T(2,128)} %param.16) | copy-start | bytes 1540
  6.5 42.0 %copy-start = (bf16[2048,512]{1,0:T(8,128)(2,1)S(1)}, bf16[2048,512]{1,0:T(8,128)(2,1)}, u32[]{:S(2)}) copy-start(bf16[2048,512]{1,0:T(8,128)(2,1)} %param.11) | copy-start | bytes 6291460
  14.5 25.2 %all-to-all-start = ((bf16[4,192,1024]{2,1,0:T(8,128)(2,1)}), bf16[4,192,1024]{2,1,0:T(8,128)(2,1)}, u32[]{:S(2)}, u32[]{:S(2)}) async-start(bf16[4,192,1024]{2,1,0:T(8,128)(2,1)} %bitcast.6), calls=%async_computation | async-start | bytes 3145728 | tf_op jit(solution)/shard_map/all_to_all | solution.py:87
  18.8 164.5 %all-gather.5.cloned.1.call-start = ((), (), s32[]{:S(2)}) async-start(), calls=%async_computation.2 | async-start | bytes 9437184 | tf_op jit(solution)/shard_map/all_gather | solution.py:108
  47.0 148.0 %all-gather.9.cloned.1.call-start = ((), (), s32[]{:S(2)}) async-start(), calls=%async_computation.4 | async-start | bytes 2621440 | tf_op jit(solution)/shard_map/all_gather | solution.py:117
  47.8 171.4 %all-gather.7.cloned.1.call-start = ((), (), s32[]{:S(2)}) async-start(), calls=%async_computation.3 | async-start | bytes 2621440 | tf_op jit(solution)/shard_map/all_gather | solution.py:118
  48.5 230.4 %all-gather.11.cloned.1.call-start = ((), (), s32[]{:S(2)}) async-start(), calls=%async_computation.5 | async-start | bytes 10485760 | tf_op jit(solution)/shard_map/all_gather | solution.py:144
  48.6 4.4 collective-permute-start
  49.1 387.9 %reduce-scatter.2.cloned.1.call-start = ((), (), s32[]{:S(2)}) async-start(), calls=%async_computation.6 | async-start | bytes 9437184 | tf_op jit(solution)/shard_map/reduce_scatter | solution.py:146
  54.9 4.5 %copy-start.1 = (s32[512]{0:T(512)S(1)}, s32[512]{0:T(512)}, u32[]{:S(2)}) copy-start(s32[512]{0:T(512)} %param.17) | copy-start | bytes 6148
  59.3 92.9 %collective-permute-start.1 = (bf16[2,2048,512]{2,1,0:T(8,128)(2,1)}, bf16[2,2048,512]{2,1,0:T(8,128)(2,1)}, u32[]{:S(2)}, u32[]{:S(2)}) collective-permute-start(bf16[2,2048,512]{2,1,0:T(8,128)(2,1)} %get-tuple-element.10), channel_id=1, source_target_pairs={{0,16},{8,24},{16,0},{24,8},{1,17},{9,25},{17,1},{25,9},{2,18},{10... | collective-permute-start | bytes 12582920 | tf_op jit(solution)/shard_map/ppermute | solution.py:22
  183.3 11.7 %copy-start.4 = (f32[8192]{0:T(1024)S(1)}, f32[8192]{0:T(1024)}, u32[]{:S(2)}) copy-start(f32[8192]{0:T(1024)} %param.10) | copy-start | bytes 98308
Sparse Core Ops, SparseCore 0:
  47.2 125.4 all-gather.4
  174.2 20.7 all-gather.8
  196.6 22.5 all-gather.6
  220.6 58.2 all-gather.10
  289.2 147.8 reduce-scatter.1
